TPU v7x, 128 devices: a whole 4x4x4 slice. The times are simulated.
128 devices in a mesh: dom: 32 (over z, y, core), sub: 4 (over x).
Axes of the slice: x: 4, y: 4, z: 4, core: 2. Of those that a mesh axis runs over, the one named last changes fastest.
Arguments:
- charges: float32 [16384, 256], P(('dom', 'sub')), may hold values from -0.3 to 0.3
- points: float32 [3, 16384, 256], P(None, ('dom', 'sub')), may hold values from -1 to 1
- leaf_basis: float32 [16384, 64, 256], P(('dom', 'sub')), may hold values from -0.375 to 0.375
- child_transfer: float32 [16384, 64, 64], P(('dom', 'sub')), may hold values from -0.75 to 0.75
- parent_transfer: float32 [2048, 64, 64], P(('dom', 'sub')), may hold values from -0.75 to 0.75
- nodes_leaf: float32 [3, 16384, 64], P(None, ('dom', 'sub')), may hold values from -2 to 2
- nodes_mid: float32 [3, 2048, 64], P(None, ('dom', 'sub')), may hold values from -2 to 2
- nodes_top: float32 [3, 256, 64], P(None, ('dom', 'sub')), may hold values from -2 to 2
- near_list: int32 [16384, 6], P(('dom', 'sub')), may hold values from -1 to 16383, as said below
- far_leaf: int32 [16384, 16], P(('dom', 'sub')), may hold values from -1 to 16383, as said below
- far_mid: int32 [2048, 16], P(('dom', 'sub')), may hold values from -1 to 2047, as said below
- far_top: int32 [256, 16], P(('dom', 'sub')), may hold values from -1 to 255, as said below
Outputs:
- potential: float32 [16384, 256], P(('dom', 'sub'))
Inputs may be any that keep to these rules, and one draw needn't show every extreme that they name: `near_list`: -1 marks an empty entry; a row's live entries come first, and its first entry is the leaf itself. Row l names only leaves of the aligned block of 128 leaves that holds l or of the blocks beside it. Some rows have all 6 entries live. `far_leaf`: -1 marks an empty entry; a row's live entries come first. Within each aligned block of 128 rows, the entries, empty ones counted, name clusters of each aligned block of 128 clusters exactly 16 times; in some row blocks all entries are live. `far_mid`: -1 marks an empty entry; a row's live entries come first. Within each aligned block of 16 rows, the entries, empty ones counted, name clusters of each aligned block of 16 clusters exactly 2 times; in some row blocks all entries are live. `far_top`: -1 marks an empty entry; a row's live entries come first; in some aligned blocks of 2 rows all entries are live.
All inputs are finite; a program needn't handle non-finite values.
Results may differ from a plain program's by a relative error of at most 0.0003.
Values sent between devices are 32-bit elements; how exact they have to be, the bound alone decides.
No kernel may reach another device: no remote copies, remote signals or barrier semaphores. Data moves between devices by JAX's collectives and lax.ppermute only.
A program may use at most 64 MiB of HBM per device.

v0:
```python
import jax
import jax.numpy as jnp
from jax import lax
from jax.sharding import PartitionSpec as P

soften = 0.25
group_rows = 32


def with_halo(cells, sides, width):
    for axis, dim in sides:
        count = lax.axis_size(axis)
        ends = count - 1
        head = lax.slice_in_dim(cells, 0, width, axis=dim)
        tail = lax.slice_in_dim(cells, cells.shape[dim] - width, cells.shape[dim], axis=dim)
        cells = jnp.concatenate(
            [
                lax.ppermute(tail, axis, [(i, (i + 1) % count) for i in range(ends)]),
                cells,
                lax.ppermute(head, axis, [((i + 1) % count, i) for i in range(ends)]),
            ],
            axis=dim,
        )
    return cells


def kernel(delta_x, delta_y, delta_z):
    return lax.rsqrt(delta_x * delta_x + delta_y * delta_y + delta_z * delta_z + soften)


def near_field(targets, table, picks_all, validity):
    row_count = targets.shape[1]
    width = targets.shape[2]
    groups = row_count // group_rows
    weights_all = validity.astype(jnp.float32)

    def one_group(group):
        start = group * group_rows
        target = lax.dynamic_slice_in_dim(targets, start, group_rows, 1)
        picks = lax.dynamic_slice_in_dim(picks_all, start, group_rows, 0)
        weights = lax.dynamic_slice_in_dim(weights_all, start, group_rows, 0)

        def one_accumulate(column, running):
            chosen = lax.dynamic_index_in_dim(picks, column, 1, keepdims=False)
            weight = lax.dynamic_index_in_dim(weights, column, 1, keepdims=False)
            nearby = jnp.take(table, chosen, axis=0)
            values = kernel(
                target[0][:, :, None] - nearby[:, None, 0:width],
                target[1][:, :, None] - nearby[:, None, width : 2 * width],
                target[2][:, :, None] - nearby[:, None, 2 * width : 3 * width],
            )
            return (
                running + jnp.sum(values * nearby[:, None, 3 * width :], axis=2) * weight[:, None]
            )

        return lax.fori_loop(
            0, picks.shape[1], one_accumulate, jnp.zeros((group_rows, width), jnp.float32)
        )

    return lax.map(one_group, jnp.arange(groups, dtype=jnp.int32)).reshape(row_count, width)


def couple(own_nodes, remote, validity):
    rank_width = own_nodes.shape[2]

    def couple_accumulate(column, running):
        piece = lax.dynamic_index_in_dim(remote, column, 1, keepdims=False)
        weight = lax.dynamic_index_in_dim(validity, column, 1, keepdims=False)
        values = kernel(
            own_nodes[0][:, :, None] - piece[:, None, rank_width : 2 * rank_width],
            own_nodes[1][:, :, None] - piece[:, None, 2 * rank_width : 3 * rank_width],
            own_nodes[2][:, :, None] - piece[:, None, 3 * rank_width :],
        )
        return running + jnp.sum(values * piece[:, None, 0:rank_width], axis=2) * weight[:, None]

    return lax.fori_loop(
        0,
        remote.shape[1],
        couple_accumulate,
        jnp.zeros((own_nodes.shape[1], rank_width), jnp.float32),
    )


def make_table(moments, nodes):
    joined = jnp.concatenate([moments[:, None, :], jnp.transpose(nodes, (1, 0, 2))], axis=1)
    return joined.reshape(moments.shape[0], -1)


def split_ids(lists, per_shard):
    entries = lists.reshape(-1)
    validity = entries >= 0
    owners = jnp.where(validity, entries // per_shard, 0)
    wanted = jnp.where(validity, entries % per_shard, 0)
    return (owners, wanted, validity)


def fetch(table, owners, wanted, validity, capacity):
    shards = lax.axis_size(("dom", "sub"))
    hit_table = (
        (owners[:, None] == jnp.arange(shards, dtype=jnp.int32)[None, :]) & validity[:, None]
    ).astype(jnp.int32)
    rank_slot = jnp.sum((jnp.cumsum(hit_table, axis=0) - 1) * hit_table, axis=1)
    places = jnp.where(validity, owners * capacity + rank_slot, shards * capacity)
    requests = (
        jnp.zeros((shards * capacity,), jnp.int32)
        .at[places]
        .set(wanted, mode="drop")
        .reshape(shards, capacity)
    )
    replies = jnp.take(
        table,
        lax.all_to_all(requests, ("dom", "sub"), split_axis=0, concat_axis=0, tiled=True),
        axis=0,
    )
    answers = lax.all_to_all(replies, ("dom", "sub"), split_axis=0, concat_axis=0, tiled=True)
    flattened = answers.reshape(shards * capacity, table.shape[1])
    return jnp.take(flattened, jnp.minimum(places, shards * capacity - 1), axis=0)


def local(
    charges,
    points,
    leaf_basis,
    child_transfer,
    parent_transfer,
    nodes_leaf,
    nodes_mid,
    nodes_top,
    near_list,
    far_leaf,
    far_mid,
    far_top,
):
    highest = lax.Precision.HIGHEST
    shards = lax.axis_size(("dom", "sub"))
    leaf_count = charges.shape[0]
    mid_count = leaf_count // 8
    top_count = mid_count // 8
    rank_width = leaf_basis.shape[1]
    fan_out = far_leaf.shape[1]
    leaf_moments = jnp.einsum("lrp,lp->lr", leaf_basis, charges, precision=highest)
    mid_moments = (
        jnp.einsum("lij,lj->li", child_transfer, leaf_moments, precision=highest)
        .reshape(mid_count, 8, rank_width)
        .sum(axis=1)
    )
    top_moments = (
        jnp.einsum("lij,lj->li", parent_transfer, mid_moments, precision=highest)
        .reshape(top_count, 8, rank_width)
        .sum(axis=1)
    )
    leaf_table = make_table(leaf_moments, nodes_leaf)
    mid_table = make_table(mid_moments, nodes_mid)
    top_table = make_table(top_moments, nodes_top)
    leaf_owner, leaf_wanted, leaf_valid = split_ids(far_leaf, leaf_count)
    mid_owner, mid_wanted, mid_valid = split_ids(far_mid, mid_count)
    cap_leaf = leaf_count * fan_out // shards
    cap_mid = mid_count * fan_out // shards
    leaf_rows = fetch(leaf_table, leaf_owner, leaf_wanted, leaf_valid, cap_leaf)
    mid_rows = fetch(mid_table, mid_owner, mid_wanted, mid_valid, cap_mid)
    every_top = lax.all_gather(top_table, ("dom", "sub"), axis=0, tiled=True)
    top_rows = jnp.take(every_top, jnp.maximum(far_top.reshape(-1), 0), axis=0)
    leaf_local = couple(
        nodes_leaf,
        leaf_rows.reshape(leaf_count, fan_out, 4 * rank_width),
        leaf_valid.reshape(leaf_count, fan_out).astype(jnp.float32),
    )
    mid_local = couple(
        nodes_mid,
        mid_rows.reshape(mid_count, fan_out, 4 * rank_width),
        mid_valid.reshape(mid_count, fan_out).astype(jnp.float32),
    )
    top_local = couple(
        nodes_top,
        top_rows.reshape(top_count, fan_out, 4 * rank_width),
        (far_top >= 0).astype(jnp.float32),
    )
    mid_down = mid_local + jnp.einsum(
        "lji,lj->li", parent_transfer, jnp.repeat(top_local, 8, axis=0), precision=highest
    )
    leaf_down = leaf_local + jnp.einsum(
        "lji,lj->li", child_transfer, jnp.repeat(mid_down, 8, axis=0), precision=highest
    )
    position = lax.axis_index(("dom", "sub"))
    point_width = charges.shape[1]
    source_rows = jnp.concatenate(
        [jnp.transpose(points, (1, 0, 2)), charges[:, None, :]], axis=1
    ).reshape(leaf_count, 4 * point_width)
    widened = with_halo(source_rows, ((("dom", "sub"), 0),), leaf_count)
    near_valid = near_list >= 0
    near_picks = jnp.where(near_valid, near_list - (position - 1) * leaf_count, 0)
    near_sum = near_field(points, widened, near_picks, near_valid)
    return jnp.einsum("lrp,lr->lp", leaf_basis, leaf_down, precision=highest) + near_sum


def solution(mesh):
    placed = (
        P(("dom", "sub"), None),
        P(None, ("dom", "sub"), None),
        P(("dom", "sub"), None, None),
        P(("dom", "sub"), None, None),
        P(("dom", "sub"), None, None),
        P(None, ("dom", "sub"), None),
        P(None, ("dom", "sub"), None),
        P(None, ("dom", "sub"), None),
        P(("dom", "sub"), None),
        P(("dom", "sub"), None),
        P(("dom", "sub"), None),
        P(("dom", "sub"), None),
    )
    return jax.shard_map(
        local, mesh=mesh, in_specs=placed, out_specs=P(("dom", "sub"), None), check_vma=False
    )
```

profile of v0, /device:TPU:1, one launch (start us, length us, event | category | flops | bytes accessed | tf_op | source)
XLA Modules:
  0.0 462.5 jit_solution(5268315734513533812)
XLA Ops:
  1.2 3.9 collective-permute-start
  5.2 3.7 collective-permute-start.1
  12.9 9.6 %all-to-all-start.2 = ((s32[128,1,2]{2,1,0:T(1,128)}), s32[128,1,2]{2,1,0:T(1,128)S(1)}, u32[]{:S(2)}, u32[]{:S(2)}) async-start(s32[128,1,2]{2,1,0:T(1,128)} %bitcast.24), calls=%async_computation.2 | async-start | bytes 131072 | tf_op jit(solution)/shard_map/all_to_all | solution.py:112
  29.9 10.3 %fusion.10 = f32[128,1,64]{2,1,0:T(1,128)} fusion(f32[128,64,256]{2,1,0:T(8,128)} %param.24, f32[128,256,1]{1,0,2:T(8,128)S(1)} %bitcast.175), kind=kOutput, calls=%fused_computation.73 | convolution fusion | flops 25165824 | bytes 8552448 | tf_op jit(solution)/shard_map/lrp,lp->lr/dot_general | solution.py:141
  44.0 1.7 multiply_reduce_fusion.5
  49.7 61.8 %all-gather = f32[128,2,256]{2,1,0:T(2,128)S(1)} all-gather(f32[1,2,256]{2,1,0:T(2,128)S(1)} %reshape.658), channel_id=1, replica_groups=mesh['dom'=32,'sub'=4] {'dom','sub'}, dimensions={0}, use_global_device_ids=true | all-gather | bytes 264192 | tf_op jit(solution)/shard_map/all_gather | solution.py:161
  114.6 6.2 %while.70 = (s32[]{:T(128)}, f32[2,64]{1,0:T(2,128)S(1)}, f32[3,2,64]{2,1,0:T(2,128)S(1)}, f32[2,16,256]{2,0,1:T(2,128)S(1)}, f32[2,16]{0,1:T(8,128)S(1)}, /*index=5*/s32[]{:T(128)}, s32[]{:T(128)}) while((s32[]{:T(128)}, f32[2,64]{1,0:T(2,128)S(1)}, f32[3,2,64]{2,1,0:T(2,128)S(1)}, f32[2,16,256]{2,0,1:T(2,128)S(1)}, ...), condition=%wide.region_18.19_spmd.clone, body=%wide.region_16.18_spmd.clone.sunk | while | flops 90371 | bytes 17015 | solution.py:76
  123.2 8.2 %scatter_custom_fusion = s32[2048]{0:T(1024)S(1)} fusion(s32[2048]{0:T(1024)} %bitcast.188, s32[2048]{0:T(1024)} %get-tuple-element.661, s32[]{:T(128)} %constant.350.clone.1), kind=kCustom, calls=%fused_computation.159 | custom fusion | bytes 8704 | tf_op jit(solution)/shard_map/scatter | solution.py:107
  133.8 6.6 %all-to-all-start = ((s32[128,1,16]{2,1,0:T(1,128)}), s32[128,1,16]{2,1,0:T(1,128)S(1)}, u32[]{:S(2)}, u32[]{:S(2)}) async-start(s32[128,1,16]{2,1,0:T(1,128)} %bitcast.8), calls=%async_computation | async-start | bytes 131072 | tf_op jit(solution)/shard_map/all_to_all | solution.py:112
  142.6 7.5 %all-to-all-done = s32[128,1,16]{2,1,0:T(1,128)S(1)} async-done(((s32[128,1,16]{2,1,0:T(1,128)}), s32[128,1,16]{2,1,0:T(1,128)S(1)}, u32[]{:S(2)}, u32[]{:S(2)}) %all-to-all-start) | async-done | bytes 8224 | tf_op jit(solution)/shard_map/all_to_all | solution.py:112
  150.1 5.1 %all-to-all-start.3 = ((f32[128,2,256]{2,1,0:T(2,128)}), f32[128,2,256]{2,1,0:T(2,128)}, u32[]{:S(2)}, u32[]{:S(2)}) async-start(f32[128,2,256]{2,1,0:T(2,128)} %broadcast_select_fusion.3), calls=%async_computation.3 | async-start | bytes 524288 | tf_op jit(solution)/shard_map/all_to_all | solution.py:115
  155.4 6.6 %gather_fusion.1 = f32[2048,256]{1,0:T(8,128)S(1)} fusion(f32[128,256]{1,0:T(8,128)S(1)} %copy.168, s32[2048]{0:T(1024)S(1)} %broadcast_clamp_fusion.1), kind=kCustom, calls=%fused_computation.1 | custom fusion | bytes 4202496 | tf_op jit(solution)/shard_map/jit(_take)/gather | solution.py:110
  163.7 2.7 all-to-all-done.3
  166.3 7.7 %all-to-all-start.1 = ((f32[128,16,256]{2,1,0:T(8,128)}), f32[128,16,256]{2,1,0:T(8,128)}, u32[]{:S(2)}, u32[]{:S(2)}) async-start(f32[128,16,256]{2,1,0:T(8,128)} %broadcast_select_fusion.2), calls=%async_computation.1 | async-start | bytes 4194304 | tf_op jit(solution)/shard_map/all_to_all | solution.py:115
  175.2 1.9 gather_fusion.4
  178.2 54.2 %while.69 = (s32[]{:T(128)}, f32[16,64]{1,0:T(8,128)S(1)}, f32[3,16,64]{2,1,0:T(8,128)}, f32[16,16,256]{2,0,1:T(8,128)S(1)}, f32[16,16]{0,1:T(8,128)}, /*index=5*/s32[]{:T(128)}, s32[]{:T(128)}) while((s32[]{:T(128)}, f32[16,64]{1,0:T(8,128)S(1)}, f32[3,16,64]{2,1,0:T(8,128)}, f32[16,16,256]{2,0,1:T(8,128)S(1)}, ...), condition=%wide.region_14.15_spmd.clone, body=%wide.region_12.14_spmd.clone.sunk | while | flops 722947 | bytes 135455 | solution.py:76
  234.9 157.7 %while.67 = (s32[]{:T(128)}, f32[4,32,256]{2,1,0:T(8,128)S(1)}, s32[4]{0:T(128)S(1)}, s32[128,6]{0,1:T(8,128)S(1)}, f32[128,6]{0,1:T(8,128)S(1)}, /*index=5*/f32...) while((s32[]{:T(128)}, f32[4,32,256]{2,1,0:T(8,128)S(1)}, ...), condition=%wide.region_23.24_spmd, body=%wide.region_19.23_spmd.sunk | while | flops 23119044 | bytes 1614134 | solution.py:60
  237.2 37.1 %while.71 = (s32[]{:T(128)}, f32[32,256]{1,0:T(8,128)S(1)}, f32[3,32,256]{2,1,0:T(8,128)S(1)}, s32[32,6]{0,1:T(8,128)S(1)}, f32[384,1024]{1,0:T(8,128)S(1)}, /*index=5*/f32[32,6]{0,1:T(8,128)S(1)}, s32[]{:T(128)}, s32[]{:T(128)}) while((s32[]{:T(128)}, f32[32,256]{1,0:T(8,128)S(1)}, f32[3,32,256]{2,1,0:T(8,128)S(1)}, ...), condition=%wide.region_22.22_spmd.clone, body=%wide.region_20.21_spmd.clone.sunk | while | flops 23119040 | bytes 1348647 | solution.py:56
  237.9 5.3 %multiply_reduce_fusion.13 = f32[32,256]{1,0:T(8,128)S(1)} fusion(f32[32,256]{1,0:T(8,128)S(1)} %get-tuple-element.908, f32[32,256]{1,0:T(8,128)S(1)} %get-tuple-element.909, f32[32,256]{1,0:T(8,128)S(1)} %get-tuple-element.910, f32[32,256]{1,0:T(8,128)S(1)} %get-tuple-element.911, f32[32,256]{1,0:T(8,128)S(1)} %get-tuple-element.912, ...), kind=kLoop, calls=%fused_computation.8.clone.1 | loop fusion | flops 23060480 | bytes 262144 | tf_op jit(solution)/shard_map/while/body/eval_jaxpr/while/body/eval_jaxpr/reduce_sum | solution.py:53
  244.1 5.3 %multiply_reduce_fusion.13 = f32[32,256]{1,0:T(8,128)S(1)} fusion(f32[32,256]{1,0:T(8,128)S(1)} %get-tuple-element.908, f32[32,256]{1,0:T(8,128)S(1)} %get-tuple-element.909, f32[32,256]{1,0:T(8,128)S(1)} %get-tuple-element.910, f32[32,256]{1,0:T(8,128)S(1)} %get-tuple-element.911, f32[32,256]{1,0:T(8,128)S(1)} %get-tuple-element.912, ...), kind=kLoop, calls=%fused_computation.8.clone.1 | loop fusion | flops 23060480 | bytes 262144 | tf_op jit(solution)/shard_map/while/body/eval_jaxpr/while/body/eval_jaxpr/reduce_sum | solution.py:53
  250.3 5.3 %multiply_reduce_fusion.13 = f32[32,256]{1,0:T(8,128)S(1)} fusion(f32[32,256]{1,0:T(8,128)S(1)} %get-tuple-element.908, f32[32,256]{1,0:T(8,128)S(1)} %get-tuple-element.909, f32[32,256]{1,0:T(8,128)S(1)} %get-tuple-element.910, f32[32,256]{1,0:T(8,128)S(1)} %get-tuple-element.911, f32[32,256]{1,0:T(8,128)S(1)} %get-tuple-element.912, ...), kind=kLoop, calls=%fused_computation.8.clone.1 | loop fusion | flops 23060480 | bytes 262144 | tf_op jit(solution)/shard_map/while/body/eval_jaxpr/while/body/eval_jaxpr/reduce_sum | solution.py:53
  256.5 5.3 %multiply_reduce_fusion.13 = f32[32,256]{1,0:T(8,128)S(1)} fusion(f32[32,256]{1,0:T(8,128)S(1)} %get-tuple-element.908, f32[32,256]{1,0:T(8,128)S(1)} %get-tuple-element.909, f32[32,256]{1,0:T(8,128)S(1)} %get-tuple-element.910, f32[32,256]{1,0:T(8,128)S(1)} %get-tuple-element.911, f32[32,256]{1,0:T(8,128)S(1)} %get-tuple-element.912, ...), kind=kLoop, calls=%fused_computation.8.clone.1 | loop fusion | flops 23060480 | bytes 262144 | tf_op jit(solution)/shard_map/while/body/eval_jaxpr/while/body/eval_jaxpr/reduce_sum | solution.py:53
  262.7 5.3 %multiply_reduce_fusion.13 = f32[32,256]{1,0:T(8,128)S(1)} fusion(f32[32,256]{1,0:T(8,128)S(1)} %get-tuple-element.908, f32[32,256]{1,0:T(8,128)S(1)} %get-tuple-element.909, f32[32,256]{1,0:T(8,128)S(1)} %get-tuple-element.910, f32[32,256]{1,0:T(8,128)S(1)} %get-tuple-element.911, f32[32,256]{1,0:T(8,128)S(1)} %get-tuple-element.912, ...), kind=kLoop, calls=%fused_computation.8.clone.1 | loop fusion | flops 23060480 | bytes 262144 | tf_op jit(solution)/shard_map/while/body/eval_jaxpr/while/body/eval_jaxpr/reduce_sum | solution.py:53
  268.9 5.3 %multiply_reduce_fusion.13 = f32[32,256]{1,0:T(8,128)S(1)} fusion(f32[32,256]{1,0:T(8,128)S(1)} %get-tuple-element.908, f32[32,256]{1,0:T(8,128)S(1)} %get-tuple-element.909, f32[32,256]{1,0:T(8,128)S(1)} %get-tuple-element.910, f32[32,256]{1,0:T(8,128)S(1)} %get-tuple-element.911, f32[32,256]{1,0:T(8,128)S(1)} %get-tuple-element.912, ...), kind=kLoop, calls=%fused_computation.8.clone.1 | loop fusion | flops 23060480 | bytes 262144 | tf_op jit(solution)/shard_map/while/body/eval_jaxpr/while/body/eval_jaxpr/reduce_sum | solution.py:53
  276.6 37.1 %while.71 = (s32[]{:T(128)}, f32[32,256]{1,0:T(8,128)S(1)}, f32[3,32,256]{2,1,0:T(8,128)S(1)}, s32[32,6]{0,1:T(8,128)S(1)}, f32[384,1024]{1,0:T(8,128)S(1)}, /*index=5*/f32[32,6]{0,1:T(8,128)S(1)}, s32[]{:T(128)}, s32[]{:T(128)}) while((s32[]{:T(128)}, f32[32,256]{1,0:T(8,128)S(1)}, f32[3,32,256]{2,1,0:T(8,128)S(1)}, ...), condition=%wide.region_22.22_spmd.clone, body=%wide.region_20.21_spmd.clone.sunk | while | flops 23119040 | bytes 1348647 | solution.py:56
  277.4 5.3 %multiply_reduce_fusion.13 = f32[32,256]{1,0:T(8,128)S(1)} fusion(f32[32,256]{1,0:T(8,128)S(1)} %get-tuple-element.908, f32[32,256]{1,0:T(8,128)S(1)} %get-tuple-element.909, f32[32,256]{1,0:T(8,128)S(1)} %get-tuple-element.910, f32[32,256]{1,0:T(8,128)S(1)} %get-tuple-element.911, f32[32,256]{1,0:T(8,128)S(1)} %get-tuple-element.912, ...), kind=kLoop, calls=%fused_computation.8.clone.1 | loop fusion | flops 23060480 | bytes 262144 | tf_op jit(solution)/shard_map/while/body/eval_jaxpr/while/body/eval_jaxpr/reduce_sum | solution.py:53
  283.6 5.3 %multiply_reduce_fusion.13 = f32[32,256]{1,0:T(8,128)S(1)} fusion(f32[32,256]{1,0:T(8,128)S(1)} %get-tuple-element.908, f32[32,256]{1,0:T(8,128)S(1)} %get-tuple-element.909, f32[32,256]{1,0:T(8,128)S(1)} %get-tuple-element.910, f32[32,256]{1,0:T(8,128)S(1)} %get-tuple-element.911, f32[32,256]{1,0:T(8,128)S(1)} %get-tuple-element.912, ...), kind=kLoop, calls=%fused_computation.8.clone.1 | loop fusion | flops 23060480 | bytes 262144 | tf_op jit(solution)/shard_map/while/body/eval_jaxpr/while/body/eval_jaxpr/reduce_sum | solution.py:53
  289.7 5.3 %multiply_reduce_fusion.13 = f32[32,256]{1,0:T(8,128)S(1)} fusion(f32[32,256]{1,0:T(8,128)S(1)} %get-tuple-element.908, f32[32,256]{1,0:T(8,128)S(1)} %get-tuple-element.909, f32[32,256]{1,0:T(8,128)S(1)} %get-tuple-element.910, f32[32,256]{1,0:T(8,128)S(1)} %get-tuple-element.911, f32[32,256]{1,0:T(8,128)S(1)} %get-tuple-element.912, ...), kind=kLoop, calls=%fused_computation.8.clone.1 | loop fusion | flops 23060480 | bytes 262144 | tf_op jit(solution)/shard_map/while/body/eval_jaxpr/while/body/eval_jaxpr/reduce_sum | solution.py:53
  295.9 5.3 %multiply_reduce_fusion.13 = f32[32,256]{1,0:T(8,128)S(1)} fusion(f32[32,256]{1,0:T(8,128)S(1)} %get-tuple-element.908, f32[32,256]{1,0:T(8,128)S(1)} %get-tuple-element.909, f32[32,256]{1,0:T(8,128)S(1)} %get-tuple-element.910, f32[32,256]{1,0:T(8,128)S(1)} %get-tuple-element.911, f32[32,256]{1,0:T(8,128)S(1)} %get-tuple-element.912, ...), kind=kLoop, calls=%fused_computation.8.clone.1 | loop fusion | flops 23060480 | bytes 262144 | tf_op jit(solution)/shard_map/while/body/eval_jaxpr/while/body/eval_jaxpr/reduce_sum | solution.py:53
  302.1 5.3 %multiply_reduce_fusion.13 = f32[32,256]{1,0:T(8,128)S(1)} fusion(f32[32,256]{1,0:T(8,128)S(1)} %get-tuple-element.908, f32[32,256]{1,0:T(8,128)S(1)} %get-tuple-element.909, f32[32,256]{1,0:T(8,128)S(1)} %get-tuple-element.910, f32[32,256]{1,0:T(8,128)S(1)} %get-tuple-element.911, f32[32,256]{1,0:T(8,128)S(1)} %get-tuple-element.912, ...), kind=kLoop, calls=%fused_computation.8.clone.1 | loop fusion | flops 23060480 | bytes 262144 | tf_op jit(solution)/shard_map/while/body/eval_jaxpr/while/body/eval_jaxpr/reduce_sum | solution.py:53
  308.3 5.3 %multiply_reduce_fusion.13 = f32[32,256]{1,0:T(8,128)S(1)} fusion(f32[32,256]{1,0:T(8,128)S(1)} %get-tuple-element.908, f32[32,256]{1,0:T(8,128)S(1)} %get-tuple-element.909, f32[32,256]{1,0:T(8,128)S(1)} %get-tuple-element.910, f32[32,256]{1,0:T(8,128)S(1)} %get-tuple-element.911, f32[32,256]{1,0:T(8,128)S(1)} %get-tuple-element.912, ...), kind=kLoop, calls=%fused_computation.8.clone.1 | loop fusion | flops 23060480 | bytes 262144 | tf_op jit(solution)/shard_map/while/body/eval_jaxpr/while/body/eval_jaxpr/reduce_sum | solution.py:53
  316.0 37.1 %while.71 = (s32[]{:T(128)}, f32[32,256]{1,0:T(8,128)S(1)}, f32[3,32,256]{2,1,0:T(8,128)S(1)}, s32[32,6]{0,1:T(8,128)S(1)}, f32[384,1024]{1,0:T(8,128)S(1)}, /*index=5*/f32[32,6]{0,1:T(8,128)S(1)}, s32[]{:T(128)}, s32[]{:T(128)}) while((s32[]{:T(128)}, f32[32,256]{1,0:T(8,128)S(1)}, f32[3,32,256]{2,1,0:T(8,128)S(1)}, ...), condition=%wide.region_22.22_spmd.clone, body=%wide.region_20.21_spmd.clone.sunk | while | flops 23119040 | bytes 1348647 | solution.py:56
  316.8 5.3 %multiply_reduce_fusion.13 = f32[32,256]{1,0:T(8,128)S(1)} fusion(f32[32,256]{1,0:T(8,128)S(1)} %get-tuple-element.908, f32[32,256]{1,0:T(8,128)S(1)} %get-tuple-element.909, f32[32,256]{1,0:T(8,128)S(1)} %get-tuple-element.910, f32[32,256]{1,0:T(8,128)S(1)} %get-tuple-element.911, f32[32,256]{1,0:T(8,128)S(1)} %get-tuple-element.912, ...), kind=kLoop, calls=%fused_computation.8.clone.1 | loop fusion | flops 23060480 | bytes 262144 | tf_op jit(solution)/shard_map/while/body/eval_jaxpr/while/body/eval_jaxpr/reduce_sum | solution.py:53
  323.0 5.3 %multiply_reduce_fusion.13 = f32[32,256]{1,0:T(8,128)S(1)} fusion(f32[32,256]{1,0:T(8,128)S(1)} %get-tuple-element.908, f32[32,256]{1,0:T(8,128)S(1)} %get-tuple-element.909, f32[32,256]{1,0:T(8,128)S(1)} %get-tuple-element.910, f32[32,256]{1,0:T(8,128)S(1)} %get-tuple-element.911, f32[32,256]{1,0:T(8,128)S(1)} %get-tuple-element.912, ...), kind=kLoop, calls=%fused_computation.8.clone.1 | loop fusion | flops 23060480 | bytes 262144 | tf_op jit(solution)/shard_map/while/body/eval_jaxpr/while/body/eval_jaxpr/reduce_sum | solution.py:53
  329.2 5.3 %multiply_reduce_fusion.13 = f32[32,256]{1,0:T(8,128)S(1)} fusion(f32[32,256]{1,0:T(8,128)S(1)} %get-tuple-element.908, f32[32,256]{1,0:T(8,128)S(1)} %get-tuple-element.909, f32[32,256]{1,0:T(8,128)S(1)} %get-tuple-element.910, f32[32,256]{1,0:T(8,128)S(1)} %get-tuple-element.911, f32[32,256]{1,0:T(8,128)S(1)} %get-tuple-element.912, ...), kind=kLoop, calls=%fused_computation.8.clone.1 | loop fusion | flops 23060480 | bytes 262144 | tf_op jit(solution)/shard_map/while/body/eval_jaxpr/while/body/eval_jaxpr/reduce_sum | solution.py:53
  335.3 5.3 %multiply_reduce_fusion.13 = f32[32,256]{1,0:T(8,128)S(1)} fusion(f32[32,256]{1,0:T(8,128)S(1)} %get-tuple-element.908, f32[32,256]{1,0:T(8,128)S(1)} %get-tuple-element.909, f32[32,256]{1,0:T(8,128)S(1)} %get-tuple-element.910, f32[32,256]{1,0:T(8,128)S(1)} %get-tuple-element.911, f32[32,256]{1,0:T(8,128)S(1)} %get-tuple-element.912, ...), kind=kLoop, calls=%fused_computation.8.clone.1 | loop fusion | flops 23060480 | bytes 262144 | tf_op jit(solution)/shard_map/while/body/eval_jaxpr/while/body/eval_jaxpr/reduce_sum | solution.py:53
  341.5 5.3 %multiply_reduce_fusion.13 = f32[32,256]{1,0:T(8,128)S(1)} fusion(f32[32,256]{1,0:T(8,128)S(1)} %get-tuple-element.908, f32[32,256]{1,0:T(8,128)S(1)} %get-tuple-element.909, f32[32,256]{1,0:T(8,128)S(1)} %get-tuple-element.910, f32[32,256]{1,0:T(8,128)S(1)} %get-tuple-element.911, f32[32,256]{1,0:T(8,128)S(1)} %get-tuple-element.912, ...), kind=kLoop, calls=%fused_computation.8.clone.1 | loop fusion | flops 23060480 | bytes 262144 | tf_op jit(solution)/shard_map/while/body/eval_jaxpr/while/body/eval_jaxpr/reduce_sum | solution.py:53
  347.7 5.3 %multiply_reduce_fusion.13 = f32[32,256]{1,0:T(8,128)S(1)} fusion(f32[32,256]{1,0:T(8,128)S(1)} %get-tuple-element.908, f32[32,256]{1,0:T(8,128)S(1)} %get-tuple-element.909, f32[32,256]{1,0:T(8,128)S(1)} %get-tuple-element.910, f32[32,256]{1,0:T(8,128)S(1)} %get-tuple-element.911, f32[32,256]{1,0:T(8,128)S(1)} %get-tuple-element.912, ...), kind=kLoop, calls=%fused_computation.8.clone.1 | loop fusion | flops 23060480 | bytes 262144 | tf_op jit(solution)/shard_map/while/body/eval_jaxpr/while/body/eval_jaxpr/reduce_sum | solution.py:53
  355.5 37.1 %while.71 = (s32[]{:T(128)}, f32[32,256]{1,0:T(8,128)S(1)}, f32[3,32,256]{2,1,0:T(8,128)S(1)}, s32[32,6]{0,1:T(8,128)S(1)}, f32[384,1024]{1,0:T(8,128)S(1)}, /*index=5*/f32[32,6]{0,1:T(8,128)S(1)}, s32[]{:T(128)}, s32[]{:T(128)}) while((s32[]{:T(128)}, f32[32,256]{1,0:T(8,128)S(1)}, f32[3,32,256]{2,1,0:T(8,128)S(1)}, ...), condition=%wide.region_22.22_spmd.clone, body=%wide.region_20.21_spmd.clone.sunk | while | flops 23119040 | bytes 1348647 | solution.py:56
  356.2 5.3 %multiply_reduce_fusion.13 = f32[32,256]{1,0:T(8,128)S(1)} fusion(f32[32,256]{1,0:T(8,128)S(1)} %get-tuple-element.908, f32[32,256]{1,0:T(8,128)S(1)} %get-tuple-element.909, f32[32,256]{1,0:T(8,128)S(1)} %get-tuple-element.910, f32[32,256]{1,0:T(8,128)S(1)} %get-tuple-element.911, f32[32,256]{1,0:T(8,128)S(1)} %get-tuple-element.912, ...), kind=kLoop, calls=%fused_computation.8.clone.1 | loop fusion | flops 23060480 | bytes 262144 | tf_op jit(solution)/shard_map/while/body/eval_jaxpr/while/body/eval_jaxpr/reduce_sum | solution.py:53
  362.4 5.3 %multiply_reduce_fusion.13 = f32[32,256]{1,0:T(8,128)S(1)} fusion(f32[32,256]{1,0:T(8,128)S(1)} %get-tuple-element.908, f32[32,256]{1,0:T(8,128)S(1)} %get-tuple-element.909, f32[32,256]{1,0:T(8,128)S(1)} %get-tuple-element.910, f32[32,256]{1,0:T(8,128)S(1)} %get-tuple-element.911, f32[32,256]{1,0:T(8,128)S(1)} %get-tuple-element.912, ...), kind=kLoop, calls=%fused_computation.8.clone.1 | loop fusion | flops 23060480 | bytes 262144 | tf_op jit(solution)/shard_map/while/body/eval_jaxpr/while/body/eval_jaxpr/reduce_sum | solution.py:53
  368.6 5.3 %multiply_reduce_fusion.13 = f32[32,256]{1,0:T(8,128)S(1)} fusion(f32[32,256]{1,0:T(8,128)S(1)} %get-tuple-element.908, f32[32,256]{1,0:T(8,128)S(1)} %get-tuple-element.909, f32[32,256]{1,0:T(8,128)S(1)} %get-tuple-element.910, f32[32,256]{1,0:T(8,128)S(1)} %get-tuple-element.911, f32[32,256]{1,0:T(8,128)S(1)} %get-tuple-element.912, ...), kind=kLoop, calls=%fused_computation.8.clone.1 | loop fusion | flops 23060480 | bytes 262144 | tf_op jit(solution)/shard_map/while/body/eval_jaxpr/while/body/eval_jaxpr/reduce_sum | solution.py:53
  374.8 5.3 %multiply_reduce_fusion.13 = f32[32,256]{1,0:T(8,128)S(1)} fusion(f32[32,256]{1,0:T(8,128)S(1)} %get-tuple-element.908, f32[32,256]{1,0:T(8,128)S(1)} %get-tuple-element.909, f32[32,256]{1,0:T(8,128)S(1)} %get-tuple-element.910, f32[32,256]{1,0:T(8,128)S(1)} %get-tuple-element.911, f32[32,256]{1,0:T(8,128)S(1)} %get-tuple-element.912, ...), kind=kLoop, calls=%fused_computation.8.clone.1 | loop fusion | flops 23060480 | bytes 262144 | tf_op jit(solution)/shard_map/while/body/eval_jaxpr/while/body/eval_jaxpr/reduce_sum | solution.py:53
  381.0 5.3 %multiply_reduce_fusion.13 = f32[32,256]{1,0:T(8,128)S(1)} fusion(f32[32,256]{1,0:T(8,128)S(1)} %get-tuple-element.908, f32[32,256]{1,0:T(8,128)S(1)} %get-tuple-element.909, f32[32,256]{1,0:T(8,128)S(1)} %get-tuple-element.910, f32[32,256]{1,0:T(8,128)S(1)} %get-tuple-element.911, f32[32,256]{1,0:T(8,128)S(1)} %get-tuple-element.912, ...), kind=kLoop, calls=%fused_computation.8.clone.1 | loop fusion | flops 23060480 | bytes 262144 | tf_op jit(solution)/shard_map/while/body/eval_jaxpr/while/body/eval_jaxpr/reduce_sum | solution.py:53
  387.1 5.3 %multiply_reduce_fusion.13 = f32[32,256]{1,0:T(8,128)S(1)} fusion(f32[32,256]{1,0:T(8,128)S(1)} %get-tuple-element.908, f32[32,256]{1,0:T(8,128)S(1)} %get-tuple-element.909, f32[32,256]{1,0:T(8,128)S(1)} %get-tuple-element.910, f32[32,256]{1,0:T(8,128)S(1)} %get-tuple-element.911, f32[32,256]{1,0:T(8,128)S(1)} %get-tuple-element.912, ...), kind=kLoop, calls=%fused_computation.8.clone.1 | loop fusion | flops 23060480 | bytes 262144 | tf_op jit(solution)/shard_map/while/body/eval_jaxpr/while/body/eval_jaxpr/reduce_sum | solution.py:53
  392.6 8.2 %gather_fusion.2 = f32[2048,256]{1,0:T(8,128)S(1)} fusion(f32[2048,256]{1,0:T(8,128)} %bitcast.16, s32[2048]{0:T(1024)S(1)} %copy-done.14), kind=kCustom, calls=%fused_computation.2 | custom fusion | bytes 4202496 | tf_op jit(solution)/shard_map/jit(_take)/gather | solution.py:117
  402.5 52.8 %while.68 = (s32[]{:T(128)}, f32[128,64]{0,1:T(8,128)S(1)}, f32[3,128,64]{1,2,0:T(8,128)S(1)}, f32[128,16,256]{2,1,0:T(8,128)}, f32[128,16]{0,1:T(8,128)}, /*index=5*/s32[]{:T(128)}, s32[]{:T(128)}) while((s32[]{:T(128)}, f32[128,64]{0,1:T(8,128)S(1)}, f32[3,128,64]{1,2,0:T(8,128)S(1)}, f32[128,16,256]{2,1,0:T(8,128)}, ...), condition=%wide.region_6.7_spmd.clone, body=%wide.region_4.6_spmd.clone.sunk | while | flops 5783555 | bytes 1345119 | solution.py:76
  455.4 6.4 %fusion.57 = f32[128,1,256]{2,1,0:T(1,128)S(1)} fusion(f32[128,64,1]{1,2,0:T(1,128)S(1)} %copy.201, f32[128,64,256]{2,1,0:T(8,128)} %param.24), kind=kOutput, calls=%fused_computation.200 | convolution fusion | flops 25165824 | bytes 8552448 | tf_op jit(solution)/shard_map/lrp,lr->lp/dot_general | solution.py:193
  (665 shorter events, 177.2 us)
Async XLA Ops:
  0.0 48.6 %copy-start = (f32[16,64,64]{2,1,0:T(8,128)S(1)}, f32[16,64,64]{2,1,0:T(8,128)}, u32[]{:S(2)}) copy-start(f32[16,64,64]{2,1,0:T(8,128)} %param.26) | copy-start | bytes 786436
  0.0 8.9 %copy-start.11 = (s32[16,16]{1,0:T(8,128)S(1)}, s32[16,16]{1,0:T(8,128)}, u32[]{:S(2)}) copy-start(s32[16,16]{1,0:T(8,128)} %param.32) | copy-start | bytes 3076
  0.0 22.6 %copy-start.16 = (s32[128,16]{0,1:T(8,128)S(1)}, s32[128,16]{0,1:T(8,128)}, u32[]{:S(2)}) copy-start(s32[128,16]{0,1:T(8,128)} %param.31) | copy-start | bytes 24580
  0.0 24.2 %copy-start.17 = (s32[2,16]{1,0:T(2,128)S(1)}, s32[2,16]{1,0:T(2,128)}, u32[]{:S(2)}) copy-start(s32[2,16]{1,0:T(2,128)} %param.33) | copy-start | bytes 388
  1.2 232.2 %collective-permute-start = (f32[128,1024]{1,0:T(8,128)S(1)}, f32[128,1024]{1,0:T(8,128)}, u32[]{:S(2)}, u32[]{:S(2)}) collective-permute-start(f32[128,1024]{1,0:T(8,128)S(1)} %bitcast.163), channel_id=1, source_target_pairs={{0,1},{1,2},{2,3},{3,4},{4,5},{5,6},{6,7},{7,8},{8,9},{9,10},{10,1... | collective-permute-start | bytes 1572872 | tf_op jit(solution)/shard_map/ppermute | solution.py:18
  5.2 228.3 %collective-permute-start.1 = (f32[128,1024]{1,0:T(8,128)S(1)}, f32[128,1024]{1,0:T(8,128)}, u32[]{:S(2)}, u32[]{:S(2)}) collective-permute-start(f32[128,1024]{1,0:T(8,128)S(1)} %bitcast.164), channel_id=1, source_target_pairs={{1,0},{2,1},{3,2},{4,3},{5,4},{6,5},{7,6},{8,7},{9,8},{10,9},{11,1... | collective-permute-start | bytes 1572872 | tf_op jit(solution)/shard_map/ppermute | solution.py:20
  12.9 120.9 %all-to-all-start.2 = ((s32[128,1,2]{2,1,0:T(1,128)}), s32[128,1,2]{2,1,0:T(1,128)S(1)}, u32[]{:S(2)}, u32[]{:S(2)}) async-start(s32[128,1,2]{2,1,0:T(1,128)} %bitcast.24), calls=%async_computation.2 | async-start | bytes 131072 | tf_op jit(solution)/shard_map/all_to_all | solution.py:112
  26.4 3.5 copy-start.5
  29.9 14.1 %copy-start.3 = (f32[3,128,64]{1,2,0:T(8,128)S(1)}, f32[3,128,64]{1,2,0:T(8,128)}, u32[]{:S(2)}) copy-start(f32[3,128,64]{1,2,0:T(8,128)} %param.27) | copy-start | bytes 294916
  29.9 14.1 %copy-start.1 = (f32[128,64,64]{0,2,1:T(8,128)S(1)}, f32[128,64,64]{0,2,1:T(8,128)}, u32[]{:S(2)}) copy-start(f32[128,64,64]{0,2,1:T(8,128)} %param.25) | copy-start | bytes 6291460
  40.2 9.3 %copy-start.12 = (f32[3,2,64]{2,1,0:T(2,128)S(1)}, f32[3,2,64]{2,1,0:T(2,128)}, u32[]{:S(2)}) copy-start(f32[3,2,64]{2,1,0:T(2,128)} %param.29) | copy-start | bytes 4612
  41.1 2.9 copy-start.6
  44.0 79.2 %copy-start.4 = (f32[3,16,64]{2,1,0:T(8,128)S(1)}, f32[3,16,64]{2,1,0:T(8,128)}, u32[]{:S(2)}) copy-start(f32[3,16,64]{2,1,0:T(8,128)} %param.28) | copy-start | bytes 36868
  45.7 76.3 %copy-start.15 = (s32[128,6]{0,1:T(8,128)S(1)}, s32[128,6]{0,1:T(8,128)}, u32[]{:S(2)}) copy-start(s32[128,6]{0,1:T(8,128)} %param.30) | copy-start | bytes 9220
  45.7 86.5 %copy-start.7 = (f32[128,16]{1,0:T(8,128)S(1)}, f32[128,16]{1,0:T(8,128)}, u32[]{:S(2)}) copy-start(f32[128,16]{1,0:T(8,128)} %get-tuple-element.657) | copy-start | bytes 24580
  133.8 16.4 %all-to-all-start = ((s32[128,1,16]{2,1,0:T(1,128)}), s32[128,1,16]{2,1,0:T(1,128)S(1)}, u32[]{:S(2)}, u32[]{:S(2)}) async-start(s32[128,1,16]{2,1,0:T(1,128)} %bitcast.8), calls=%async_computation | async-start | bytes 131072 | tf_op jit(solution)/shard_map/all_to_all | solution.py:112
  150.1 16.2 %all-to-all-start.3 = ((f32[128,2,256]{2,1,0:T(2,128)}), f32[128,2,256]{2,1,0:T(2,128)}, u32[]{:S(2)}, u32[]{:S(2)}) async-start(f32[128,2,256]{2,1,0:T(2,128)} %broadcast_select_fusion.3), calls=%async_computation.3 | async-start | bytes 524288 | tf_op jit(solution)/shard_map/all_to_all | solution.py:115
  166.3 226.2 %all-to-all-start.1 = ((f32[128,16,256]{2,1,0:T(8,128)}), f32[128,16,256]{2,1,0:T(8,128)}, u32[]{:S(2)}, u32[]{:S(2)}) async-start(f32[128,16,256]{2,1,0:T(8,128)} %broadcast_select_fusion.2), calls=%async_computation.1 | async-start | bytes 4194304 | tf_op jit(solution)/shard_map/all_to_all | solution.py:115
  175.2 58.1 %copy-start.2 = (f32[128,64,64]{0,2,1:T(8,128)S(1)}, f32[128,64,64]{0,2,1:T(8,128)}, u32[]{:S(2)}) copy-start(f32[128,64,64]{0,2,1:T(8,128)} %param.25) | copy-start | bytes 6291460
  233.4 1.4 copy-start.8
  233.4 1.4 copy-start.9
  233.4 1.4 copy-start.10
  234.9 157.7 %copy-start.14 = (s32[2048]{0:T(1024)S(1)}, s32[2048]{0:T(1024)}, u32[]{:S(2)}) copy-start(s32[2048]{0:T(1024)} %broadcast_clamp_fusion) | copy-start | bytes 24580
  392.6 8.3 %copy-start.13 = (pred[128,16]{1,0:T(8,128)(4,1)S(1)}, pred[128,16]{1,0:T(8,128)(4,1)}, u32[]{:S(2)}) copy-start(pred[128,16]{1,0:T(8,128)(4,1)} %get-tuple-element.658) | copy-start | bytes 6148
where the time goes:
time: 466 us; the launch traced here: 463 us
  other arithmetic  199 us (43%)
  local copies, waits for them, and re-layouts  130 us (28%)
  blocking collectives  61.8 us (13%)
  starting transfers between devices  36.7 us (8%)
  matrix products  18.8 us (4%)
  waiting for transfers between devices  10.2 us (2%)
  loops' own time  5.1 us (1%)
    reduce_sum x24, other arithmetic, one_accumulate(): jnp.sum(values * nearby[:, None, 3 * width:], axis=2) * weight[:, None]  128 us
    all_gather x1, blocking collectives, local(): every_top = lax.all_gather(top_table, ('dom', 'sub'), axis=0, tiled=True)  61.8 us
    reduce_sum x48, other arithmetic, couple_accumulate(): jnp.sum(values * piece[:, None, 0:rank_width], axis=2) * weight[:, None]  31.9 us
    mul x48, local copies, waits for them, and re-layouts, couple_accumulate(): jnp.sum(values * piece[:, None, 0:rank_width], axis=2) * weight[:, None]  30.5 us
    dynamic_slice x32, local copies, waits for them, and re-layouts, couple_accumulate(): piece = lax.dynamic_index_in_dim(remote, column, 1, keepdims=False)  22.7 us
    all_to_all x2, starting transfers between devices, fetch(): lax.all_to_all(requests, ('dom', 'sub'), split_axis=0, concat_axis=0, til...  16.3 us
    gather x24, local copies, waits for them, and re-layouts, one_accumulate(): nearby = jnp.take(table, chosen, axis=0)  14.8 us
    all_to_all x2, starting transfers between devices, fetch(): lax.all_to_all(replies, ('dom', 'sub'), split_axis=0, concat_axis=0, tile...  12.8 us
  transfers between devices with their start and end apart: 6, of which 2 were waited for; matrix products, arithmetic and copies ran while one was open for 60% of the time, Pallas kernels for 0%

commit v1 on v0

--- a/solution.py
+++ b/solution.py
@@ -158,7 +158,12 @@
     cap_mid = mid_count * fan_out // shards
     leaf_rows = fetch(leaf_table, leaf_owner, leaf_wanted, leaf_valid, cap_leaf)
     mid_rows = fetch(mid_table, mid_owner, mid_wanted, mid_valid, cap_mid)
-    every_top = lax.all_gather(top_table, ("dom", "sub"), axis=0, tiled=True)
+    every_top = jnp.concatenate(
+        lax.all_to_all(
+            jnp.stack([top_table] * lax.axis_size(("dom", "sub"))), ("dom", "sub"), 0, 0
+        ),
+        axis=0,
+    )
     top_rows = jnp.take(every_top, jnp.maximum(far_top.reshape(-1), 0), axis=0)
     leaf_local = couple(
         nodes_leaf,

time: 466 us -> 419 us (0.90)
  blocking collectives: 61.8 us -> 0 us
  starting transfers between devices: 36.7 us -> 47.5 us
    all_gather x1 -> x0, blocking collectives: 61.8 us -> none  [local(): every_top = lax.all_gather(top_table, ('dom', 'sub'), axis=0, tiled=True)]
    all_to_all x0 -> x1, starting transfers between devices: none -> 5.07 us  [local(): lax.all_to_all(jnp.stack([top_table] * lax.axis_size(('dom', 'sub'))), ('...]
  transfers between devices with their start and end apart: 6 -> 7, of which waited for: 2 -> 3; matrix products, arithmetic and copies ran while one was open for 60% -> 67% of each run, Pallas kernels for 0% -> 0%
where the time goes in v1:
time: 419 us; the launch traced here: 415 us
  other arithmetic  199 us (47%)
  local copies, waits for them, and re-layouts  131 us (31%)
  starting transfers between devices  47.5 us (11%)
  matrix products  19.1 us (5%)
  waiting for transfers between devices  12.3 us (3%)
  loops' own time  5.1 us (1%)
    reduce_sum x24, other arithmetic, one_accumulate(): jnp.sum(values * nearby[:, None, 3 * width:], axis=2) * weight[:, None]  128 us
    reduce_sum x48, other arithmetic, couple_accumulate(): jnp.sum(values * piece[:, None, 0:rank_width], axis=2) * weight[:, None]  31.9 us
    mul x48, local copies, waits for them, and re-layouts, couple_accumulate(): jnp.sum(values * piece[:, None, 0:rank_width], axis=2) * weight[:, None]  30.4 us
    dynamic_slice x32, local copies, waits for them, and re-layouts, couple_accumulate(): piece = lax.dynamic_index_in_dim(remote, column, 1, keepdims=False)  22.7 us
    all_to_all x2, starting transfers between devices, fetch(): lax.all_to_all(requests, ('dom', 'sub'), split_axis=0, concat_axis=0, til...  19.4 us
    all_to_all x2, starting transfers between devices, fetch(): lax.all_to_all(replies, ('dom', 'sub'), split_axis=0, concat_axis=0, tile...  15.3 us
    gather x24, local copies, waits for them, and re-layouts, one_accumulate(): nearby = jnp.take(table, chosen, axis=0)  14.8 us
    add x48, other arithmetic, couple_accumulate(): running + jnp.sum(values * piece[:, None, 0:rank_width], axis=2) * weight...  12.4 us
  transfers between devices with their start and end apart: 7, of which 3 were waited for; matrix products, arithmetic and copies ran while one was open for 67% of the time, Pallas kernels for 0%

profile of v1, /device:TPU:1, one launch (start us, length us, event | category | flops | bytes accessed | tf_op | source)
XLA Modules:
  0.0 415.1 jit_solution(13737973621628310384)
XLA Ops:
  1.2 3.9 collective-permute-start
  5.2 3.7 collective-permute-start.1
  12.9 9.6 %all-to-all-start.2 = ((s32[128,1,2]{2,1,0:T(1,128)}), s32[128,1,2]{2,1,0:T(1,128)S(1)}, u32[]{:S(2)}, u32[]{:S(2)}) async-start(s32[128,1,2]{2,1,0:T(1,128)} %bitcast.24), calls=%async_computation.2 | async-start | bytes 131072 | tf_op jit(solution)/shard_map/all_to_all | solution.py:112
  29.9 10.6 %fusion.10 = f32[128,1,64]{2,1,0:T(1,128)S(1)} fusion(f32[128,64,256]{2,1,0:T(8,128)} %param.24, f32[128,256,1]{1,0,2:T(8,128)} %bitcast.175), kind=kOutput, calls=%fused_computation.73 | convolution fusion | flops 25165824 | bytes 8552448 | tf_op jit(solution)/shard_map/lrp,lp->lr/dot_general | solution.py:141
  50.1 8.2 %scatter_custom_fusion = s32[2048]{0:T(1024)S(1)} fusion(s32[2048]{0:T(1024)} %bitcast.188, s32[2048]{0:T(1024)} %get-tuple-element.661, s32[]{:T(128)} %constant.350.clone.1), kind=kCustom, calls=%fused_computation.159 | custom fusion | bytes 8704 | tf_op jit(solution)/shard_map/scatter | solution.py:107
  64.5 9.8 %all-to-all-start = ((s32[128,1,16]{2,1,0:T(1,128)}), s32[128,1,16]{2,1,0:T(1,128)S(1)}, u32[]{:S(2)}, u32[]{:S(2)}) async-start(s32[128,1,16]{2,1,0:T(1,128)} %bitcast.8), calls=%async_computation | async-start | bytes 131072 | tf_op jit(solution)/shard_map/all_to_all | solution.py:112
  76.5 7.5 %all-to-all-done = s32[128,1,16]{2,1,0:T(1,128)S(1)} async-done(((s32[128,1,16]{2,1,0:T(1,128)}), s32[128,1,16]{2,1,0:T(1,128)S(1)}, u32[]{:S(2)}, u32[]{:S(2)}) %all-to-all-start) | async-done | bytes 8224 | tf_op jit(solution)/shard_map/all_to_all | solution.py:112
  84.7 5.1 %all-to-all-start.4 = ((f32[128,2,256]{2,1,0:T(2,128)}), f32[128,2,256]{2,1,0:T(2,128)}, u32[]{:S(2)}, u32[]{:S(2)}) async-start(f32[128,2,256]{2,1,0:T(2,128)} %stack.3), calls=%async_computation.4 | async-start | bytes 524288 | tf_op jit(solution)/shard_map/all_to_all | solution.py:162
  89.9 6.6 %gather_fusion.1 = f32[2048,256]{1,0:T(8,128)S(1)} fusion(f32[128,256]{1,0:T(8,128)S(1)} %copy.168, s32[2048]{0:T(1024)S(1)} %broadcast_clamp_fusion.1), kind=kCustom, calls=%fused_computation.1 | custom fusion | bytes 4202496 | tf_op jit(solution)/shard_map/jit(_take)/gather | solution.py:110
  98.3 2.7 all-to-all-done.4
  100.9 7.2 %all-to-all-start.3 = ((f32[128,2,256]{2,1,0:T(2,128)}), f32[128,2,256]{2,1,0:T(2,128)S(1)}, u32[]{:S(2)}, u32[]{:S(2)}) async-start(f32[128,2,256]{2,1,0:T(2,128)} %broadcast_select_fusion.3), calls=%async_computation.3 | async-start | bytes 524288 | tf_op jit(solution)/shard_map/all_to_all | solution.py:115
  110.0 6.2 %while.70 = (s32[]{:T(128)}, f32[2,64]{1,0:T(2,128)S(1)}, f32[3,2,64]{2,1,0:T(2,128)S(1)}, f32[2,16,256]{2,0,1:T(2,128)S(1)}, f32[2,16]{0,1:T(8,128)S(1)}, /*index=5*/s32[]{:T(128)}, s32[]{:T(128)}) while((s32[]{:T(128)}, f32[2,64]{1,0:T(2,128)S(1)}, f32[3,2,64]{2,1,0:T(2,128)S(1)}, f32[2,16,256]{2,0,1:T(2,128)S(1)}, ...), condition=%wide.region_18.19_spmd.clone, body=%wide.region_16.18_spmd.clone.sunk | while | flops 90371 | bytes 17015 | solution.py:76
  117.4 2.2 all-to-all-done.3
  119.5 8.1 %all-to-all-start.1 = ((f32[128,16,256]{2,1,0:T(8,128)}), f32[128,16,256]{2,1,0:T(8,128)}, u32[]{:S(2)}, u32[]{:S(2)}) async-start(f32[128,16,256]{2,1,0:T(8,128)} %broadcast_select_fusion.2), calls=%async_computation.1 | async-start | bytes 4194304 | tf_op jit(solution)/shard_map/all_to_all | solution.py:115
  127.8 1.9 gather_fusion.4
  130.9 54.1 %while.69 = (s32[]{:T(128)}, f32[16,64]{1,0:T(8,128)S(1)}, f32[3,16,64]{2,1,0:T(8,128)}, f32[16,16,256]{2,0,1:T(8,128)S(1)}, f32[16,16]{0,1:T(8,128)}, /*index=5*/s32[]{:T(128)}, s32[]{:T(128)}) while((s32[]{:T(128)}, f32[16,64]{1,0:T(8,128)S(1)}, f32[3,16,64]{2,1,0:T(8,128)}, f32[16,16,256]{2,0,1:T(8,128)S(1)}, ...), condition=%wide.region_14.15_spmd.clone, body=%wide.region_12.14_spmd.clone.sunk | while | flops 722947 | bytes 135455 | solution.py:76
  187.4 157.7 %while.67 = (s32[]{:T(128)}, f32[4,32,256]{2,1,0:T(8,128)S(1)}, s32[4]{0:T(128)S(1)}, s32[128,6]{0,1:T(8,128)S(1)}, f32[128,6]{0,1:T(8,128)S(1)}, /*index=5*/f32...) while((s32[]{:T(128)}, f32[4,32,256]{2,1,0:T(8,128)S(1)}, ...), condition=%wide.region_23.24_spmd, body=%wide.region_19.23_spmd.sunk | while | flops 23119044 | bytes 1614134 | solution.py:60
  189.7 37.1 %while.71 = (s32[]{:T(128)}, f32[32,256]{1,0:T(8,128)S(1)}, f32[3,32,256]{2,1,0:T(8,128)S(1)}, s32[32,6]{0,1:T(8,128)S(1)}, f32[384,1024]{1,0:T(8,128)S(1)}, /*index=5*/f32[32,6]{0,1:T(8,128)S(1)}, s32[]{:T(128)}, s32[]{:T(128)}) while((s32[]{:T(128)}, f32[32,256]{1,0:T(8,128)S(1)}, f32[3,32,256]{2,1,0:T(8,128)S(1)}, ...), condition=%wide.region_22.22_spmd.clone, body=%wide.region_20.21_spmd.clone.sunk | while | flops 23119040 | bytes 1348647 | solution.py:56
  190.5 5.3 %multiply_reduce_fusion.13 = f32[32,256]{1,0:T(8,128)S(1)} fusion(f32[32,256]{1,0:T(8,128)S(1)} %get-tuple-element.908, f32[32,256]{1,0:T(8,128)S(1)} %get-tuple-element.909, f32[32,256]{1,0:T(8,128)S(1)} %get-tuple-element.910, f32[32,256]{1,0:T(8,128)S(1)} %get-tuple-element.911, f32[32,256]{1,0:T(8,128)S(1)} %get-tuple-element.912, ...), kind=kLoop, calls=%fused_computation.8.clone.1 | loop fusion | flops 23060480 | bytes 262144 | tf_op jit(solution)/shard_map/while/body/eval_jaxpr/while/body/eval_jaxpr/reduce_sum | solution.py:53
  196.7 5.3 %multiply_reduce_fusion.13 = f32[32,256]{1,0:T(8,128)S(1)} fusion(f32[32,256]{1,0:T(8,128)S(1)} %get-tuple-element.908, f32[32,256]{1,0:T(8,128)S(1)} %get-tuple-element.909, f32[32,256]{1,0:T(8,128)S(1)} %get-tuple-element.910, f32[32,256]{1,0:T(8,128)S(1)} %get-tuple-element.911, f32[32,256]{1,0:T(8,128)S(1)} %get-tuple-element.912, ...), kind=kLoop, calls=%fused_computation.8.clone.1 | loop fusion | flops 23060480 | bytes 262144 | tf_op jit(solution)/shard_map/while/body/eval_jaxpr/while/body/eval_jaxpr/reduce_sum | solution.py:53
  202.9 5.3 %multiply_reduce_fusion.13 = f32[32,256]{1,0:T(8,128)S(1)} fusion(f32[32,256]{1,0:T(8,128)S(1)} %get-tuple-element.908, f32[32,256]{1,0:T(8,128)S(1)} %get-tuple-element.909, f32[32,256]{1,0:T(8,128)S(1)} %get-tuple-element.910, f32[32,256]{1,0:T(8,128)S(1)} %get-tuple-element.911, f32[32,256]{1,0:T(8,128)S(1)} %get-tuple-element.912, ...), kind=kLoop, calls=%fused_computation.8.clone.1 | loop fusion | flops 23060480 | bytes 262144 | tf_op jit(solution)/shard_map/while/body/eval_jaxpr/while/body/eval_jaxpr/reduce_sum | solution.py:53
  209.0 5.3 %multiply_reduce_fusion.13 = f32[32,256]{1,0:T(8,128)S(1)} fusion(f32[32,256]{1,0:T(8,128)S(1)} %get-tuple-element.908, f32[32,256]{1,0:T(8,128)S(1)} %get-tuple-element.909, f32[32,256]{1,0:T(8,128)S(1)} %get-tuple-element.910, f32[32,256]{1,0:T(8,128)S(1)} %get-tuple-element.911, f32[32,256]{1,0:T(8,128)S(1)} %get-tuple-element.912, ...), kind=kLoop, calls=%fused_computation.8.clone.1 | loop fusion | flops 23060480 | bytes 262144 | tf_op jit(solution)/shard_map/while/body/eval_jaxpr/while/body/eval_jaxpr/reduce_sum | solution.py:53
  215.2 5.3 %multiply_reduce_fusion.13 = f32[32,256]{1,0:T(8,128)S(1)} fusion(f32[32,256]{1,0:T(8,128)S(1)} %get-tuple-element.908, f32[32,256]{1,0:T(8,128)S(1)} %get-tuple-element.909, f32[32,256]{1,0:T(8,128)S(1)} %get-tuple-element.910, f32[32,256]{1,0:T(8,128)S(1)} %get-tuple-element.911, f32[32,256]{1,0:T(8,128)S(1)} %get-tuple-element.912, ...), kind=kLoop, calls=%fused_computation.8.clone.1 | loop fusion | flops 23060480 | bytes 262144 | tf_op jit(solution)/shard_map/while/body/eval_jaxpr/while/body/eval_jaxpr/reduce_sum | solution.py:53
  221.4 5.3 %multiply_reduce_fusion.13 = f32[32,256]{1,0:T(8,128)S(1)} fusion(f32[32,256]{1,0:T(8,128)S(1)} %get-tuple-element.908, f32[32,256]{1,0:T(8,128)S(1)} %get-tuple-element.909, f32[32,256]{1,0:T(8,128)S(1)} %get-tuple-element.910, f32[32,256]{1,0:T(8,128)S(1)} %get-tuple-element.911, f32[32,256]{1,0:T(8,128)S(1)} %get-tuple-element.912, ...), kind=kLoop, calls=%fused_computation.8.clone.1 | loop fusion | flops 23060480 | bytes 262144 | tf_op jit(solution)/shard_map/while/body/eval_jaxpr/while/body/eval_jaxpr/reduce_sum | solution.py:53
  229.2 37.1 %while.71 = (s32[]{:T(128)}, f32[32,256]{1,0:T(8,128)S(1)}, f32[3,32,256]{2,1,0:T(8,128)S(1)}, s32[32,6]{0,1:T(8,128)S(1)}, f32[384,1024]{1,0:T(8,128)S(1)}, /*index=5*/f32[32,6]{0,1:T(8,128)S(1)}, s32[]{:T(128)}, s32[]{:T(128)}) while((s32[]{:T(128)}, f32[32,256]{1,0:T(8,128)S(1)}, f32[3,32,256]{2,1,0:T(8,128)S(1)}, ...), condition=%wide.region_22.22_spmd.clone, body=%wide.region_20.21_spmd.clone.sunk | while | flops 23119040 | bytes 1348647 | solution.py:56
  229.9 5.3 %multiply_reduce_fusion.13 = f32[32,256]{1,0:T(8,128)S(1)} fusion(f32[32,256]{1,0:T(8,128)S(1)} %get-tuple-element.908, f32[32,256]{1,0:T(8,128)S(1)} %get-tuple-element.909, f32[32,256]{1,0:T(8,128)S(1)} %get-tuple-element.910, f32[32,256]{1,0:T(8,128)S(1)} %get-tuple-element.911, f32[32,256]{1,0:T(8,128)S(1)} %get-tuple-element.912, ...), kind=kLoop, calls=%fused_computation.8.clone.1 | loop fusion | flops 23060480 | bytes 262144 | tf_op jit(solution)/shard_map/while/body/eval_jaxpr/while/body/eval_jaxpr/reduce_sum | solution.py:53
  236.1 5.3 %multiply_reduce_fusion.13 = f32[32,256]{1,0:T(8,128)S(1)} fusion(f32[32,256]{1,0:T(8,128)S(1)} %get-tuple-element.908, f32[32,256]{1,0:T(8,128)S(1)} %get-tuple-element.909, f32[32,256]{1,0:T(8,128)S(1)} %get-tuple-element.910, f32[32,256]{1,0:T(8,128)S(1)} %get-tuple-element.911, f32[32,256]{1,0:T(8,128)S(1)} %get-tuple-element.912, ...), kind=kLoop, calls=%fused_computation.8.clone.1 | loop fusion | flops 23060480 | bytes 262144 | tf_op jit(solution)/shard_map/while/body/eval_jaxpr/while/body/eval_jaxpr/reduce_sum | solution.py:53
  242.3 5.3 %multiply_reduce_fusion.13 = f32[32,256]{1,0:T(8,128)S(1)} fusion(f32[32,256]{1,0:T(8,128)S(1)} %get-tuple-element.908, f32[32,256]{1,0:T(8,128)S(1)} %get-tuple-element.909, f32[32,256]{1,0:T(8,128)S(1)} %get-tuple-element.910, f32[32,256]{1,0:T(8,128)S(1)} %get-tuple-element.911, f32[32,256]{1,0:T(8,128)S(1)} %get-tuple-element.912, ...), kind=kLoop, calls=%fused_computation.8.clone.1 | loop fusion | flops 23060480 | bytes 262144 | tf_op jit(solution)/shard_map/while/body/eval_jaxpr/while/body/eval_jaxpr/reduce_sum | solution.py:53
  248.5 5.3 %multiply_reduce_fusion.13 = f32[32,256]{1,0:T(8,128)S(1)} fusion(f32[32,256]{1,0:T(8,128)S(1)} %get-tuple-element.908, f32[32,256]{1,0:T(8,128)S(1)} %get-tuple-element.909, f32[32,256]{1,0:T(8,128)S(1)} %get-tuple-element.910, f32[32,256]{1,0:T(8,128)S(1)} %get-tuple-element.911, f32[32,256]{1,0:T(8,128)S(1)} %get-tuple-element.912, ...), kind=kLoop, calls=%fused_computation.8.clone.1 | loop fusion | flops 23060480 | bytes 262144 | tf_op jit(solution)/shard_map/while/body/eval_jaxpr/while/body/eval_jaxpr/reduce_sum | solution.py:53
  254.7 5.3 %multiply_reduce_fusion.13 = f32[32,256]{1,0:T(8,128)S(1)} fusion(f32[32,256]{1,0:T(8,128)S(1)} %get-tuple-element.908, f32[32,256]{1,0:T(8,128)S(1)} %get-tuple-element.909, f32[32,256]{1,0:T(8,128)S(1)} %get-tuple-element.910, f32[32,256]{1,0:T(8,128)S(1)} %get-tuple-element.911, f32[32,256]{1,0:T(8,128)S(1)} %get-tuple-element.912, ...), kind=kLoop, calls=%fused_computation.8.clone.1 | loop fusion | flops 23060480 | bytes 262144 | tf_op jit(solution)/shard_map/while/body/eval_jaxpr/while/body/eval_jaxpr/reduce_sum | solution.py:53
  260.8 5.3 %multiply_reduce_fusion.13 = f32[32,256]{1,0:T(8,128)S(1)} fusion(f32[32,256]{1,0:T(8,128)S(1)} %get-tuple-element.908, f32[32,256]{1,0:T(8,128)S(1)} %get-tuple-element.909, f32[32,256]{1,0:T(8,128)S(1)} %get-tuple-element.910, f32[32,256]{1,0:T(8,128)S(1)} %get-tuple-element.911, f32[32,256]{1,0:T(8,128)S(1)} %get-tuple-element.912, ...), kind=kLoop, calls=%fused_computation.8.clone.1 | loop fusion | flops 23060480 | bytes 262144 | tf_op jit(solution)/shard_map/while/body/eval_jaxpr/while/body/eval_jaxpr/reduce_sum | solution.py:53
  268.6 37.1 %while.71 = (s32[]{:T(128)}, f32[32,256]{1,0:T(8,128)S(1)}, f32[3,32,256]{2,1,0:T(8,128)S(1)}, s32[32,6]{0,1:T(8,128)S(1)}, f32[384,1024]{1,0:T(8,128)S(1)}, /*index=5*/f32[32,6]{0,1:T(8,128)S(1)}, s32[]{:T(128)}, s32[]{:T(128)}) while((s32[]{:T(128)}, f32[32,256]{1,0:T(8,128)S(1)}, f32[3,32,256]{2,1,0:T(8,128)S(1)}, ...), condition=%wide.region_22.22_spmd.clone, body=%wide.region_20.21_spmd.clone.sunk | while | flops 23119040 | bytes 1348647 | solution.py:56
  269.3 5.3 %multiply_reduce_fusion.13 = f32[32,256]{1,0:T(8,128)S(1)} fusion(f32[32,256]{1,0:T(8,128)S(1)} %get-tuple-element.908, f32[32,256]{1,0:T(8,128)S(1)} %get-tuple-element.909, f32[32,256]{1,0:T(8,128)S(1)} %get-tuple-element.910, f32[32,256]{1,0:T(8,128)S(1)} %get-tuple-element.911, f32[32,256]{1,0:T(8,128)S(1)} %get-tuple-element.912, ...), kind=kLoop, calls=%fused_computation.8.clone.1 | loop fusion | flops 23060480 | bytes 262144 | tf_op jit(solution)/shard_map/while/body/eval_jaxpr/while/body/eval_jaxpr/reduce_sum | solution.py:53
  275.5 5.3 %multiply_reduce_fusion.13 = f32[32,256]{1,0:T(8,128)S(1)} fusion(f32[32,256]{1,0:T(8,128)S(1)} %get-tuple-element.908, f32[32,256]{1,0:T(8,128)S(1)} %get-tuple-element.909, f32[32,256]{1,0:T(8,128)S(1)} %get-tuple-element.910, f32[32,256]{1,0:T(8,128)S(1)} %get-tuple-element.911, f32[32,256]{1,0:T(8,128)S(1)} %get-tuple-element.912, ...), kind=kLoop, calls=%fused_computation.8.clone.1 | loop fusion | flops 23060480 | bytes 262144 | tf_op jit(solution)/shard_map/while/body/eval_jaxpr/while/body/eval_jaxpr/reduce_sum | solution.py:53
  281.7 5.3 %multiply_reduce_fusion.13 = f32[32,256]{1,0:T(8,128)S(1)} fusion(f32[32,256]{1,0:T(8,128)S(1)} %get-tuple-element.908, f32[32,256]{1,0:T(8,128)S(1)} %get-tuple-element.909, f32[32,256]{1,0:T(8,128)S(1)} %get-tuple-element.910, f32[32,256]{1,0:T(8,128)S(1)} %get-tuple-element.911, f32[32,256]{1,0:T(8,128)S(1)} %get-tuple-element.912, ...), kind=kLoop, calls=%fused_computation.8.clone.1 | loop fusion | flops 23060480 | bytes 262144 | tf_op jit(solution)/shard_map/while/body/eval_jaxpr/while/body/eval_jaxpr/reduce_sum | solution.py:53
  287.9 5.3 %multiply_reduce_fusion.13 = f32[32,256]{1,0:T(8,128)S(1)} fusion(f32[32,256]{1,0:T(8,128)S(1)} %get-tuple-element.908, f32[32,256]{1,0:T(8,128)S(1)} %get-tuple-element.909, f32[32,256]{1,0:T(8,128)S(1)} %get-tuple-element.910, f32[32,256]{1,0:T(8,128)S(1)} %get-tuple-element.911, f32[32,256]{1,0:T(8,128)S(1)} %get-tuple-element.912, ...), kind=kLoop, calls=%fused_computation.8.clone.1 | loop fusion | flops 23060480 | bytes 262144 | tf_op jit(solution)/shard_map/while/body/eval_jaxpr/while/body/eval_jaxpr/reduce_sum | solution.py:53
  294.1 5.3 %multiply_reduce_fusion.13 = f32[32,256]{1,0:T(8,128)S(1)} fusion(f32[32,256]{1,0:T(8,128)S(1)} %get-tuple-element.908, f32[32,256]{1,0:T(8,128)S(1)} %get-tuple-element.909, f32[32,256]{1,0:T(8,128)S(1)} %get-tuple-element.910, f32[32,256]{1,0:T(8,128)S(1)} %get-tuple-element.911, f32[32,256]{1,0:T(8,128)S(1)} %get-tuple-element.912, ...), kind=kLoop, calls=%fused_computation.8.clone.1 | loop fusion | flops 23060480 | bytes 262144 | tf_op jit(solution)/shard_map/while/body/eval_jaxpr/while/body/eval_jaxpr/reduce_sum | solution.py:53
  300.3 5.3 %multiply_reduce_fusion.13 = f32[32,256]{1,0:T(8,128)S(1)} fusion(f32[32,256]{1,0:T(8,128)S(1)} %get-tuple-element.908, f32[32,256]{1,0:T(8,128)S(1)} %get-tuple-element.909, f32[32,256]{1,0:T(8,128)S(1)} %get-tuple-element.910, f32[32,256]{1,0:T(8,128)S(1)} %get-tuple-element.911, f32[32,256]{1,0:T(8,128)S(1)} %get-tuple-element.912, ...), kind=kLoop, calls=%fused_computation.8.clone.1 | loop fusion | flops 23060480 | bytes 262144 | tf_op jit(solution)/shard_map/while/body/eval_jaxpr/while/body/eval_jaxpr/reduce_sum | solution.py:53
  308.0 37.1 %while.71 = (s32[]{:T(128)}, f32[32,256]{1,0:T(8,128)S(1)}, f32[3,32,256]{2,1,0:T(8,128)S(1)}, s32[32,6]{0,1:T(8,128)S(1)}, f32[384,1024]{1,0:T(8,128)S(1)}, /*index=5*/f32[32,6]{0,1:T(8,128)S(1)}, s32[]{:T(128)}, s32[]{:T(128)}) while((s32[]{:T(128)}, f32[32,256]{1,0:T(8,128)S(1)}, f32[3,32,256]{2,1,0:T(8,128)S(1)}, ...), condition=%wide.region_22.22_spmd.clone, body=%wide.region_20.21_spmd.clone.sunk | while | flops 23119040 | bytes 1348647 | solution.py:56
  308.8 5.3 %multiply_reduce_fusion.13 = f32[32,256]{1,0:T(8,128)S(1)} fusion(f32[32,256]{1,0:T(8,128)S(1)} %get-tuple-element.908, f32[32,256]{1,0:T(8,128)S(1)} %get-tuple-element.909, f32[32,256]{1,0:T(8,128)S(1)} %get-tuple-element.910, f32[32,256]{1,0:T(8,128)S(1)} %get-tuple-element.911, f32[32,256]{1,0:T(8,128)S(1)} %get-tuple-element.912, ...), kind=kLoop, calls=%fused_computation.8.clone.1 | loop fusion | flops 23060480 | bytes 262144 | tf_op jit(solution)/shard_map/while/body/eval_jaxpr/while/body/eval_jaxpr/reduce_sum | solution.py:53
  315.0 5.3 %multiply_reduce_fusion.13 = f32[32,256]{1,0:T(8,128)S(1)} fusion(f32[32,256]{1,0:T(8,128)S(1)} %get-tuple-element.908, f32[32,256]{1,0:T(8,128)S(1)} %get-tuple-element.909, f32[32,256]{1,0:T(8,128)S(1)} %get-tuple-element.910, f32[32,256]{1,0:T(8,128)S(1)} %get-tuple-element.911, f32[32,256]{1,0:T(8,128)S(1)} %get-tuple-element.912, ...), kind=kLoop, calls=%fused_computation.8.clone.1 | loop fusion | flops 23060480 | bytes 262144 | tf_op jit(solution)/shard_map/while/body/eval_jaxpr/while/body/eval_jaxpr/reduce_sum | solution.py:53
  321.1 5.3 %multiply_reduce_fusion.13 = f32[32,256]{1,0:T(8,128)S(1)} fusion(f32[32,256]{1,0:T(8,128)S(1)} %get-tuple-element.908, f32[32,256]{1,0:T(8,128)S(1)} %get-tuple-element.909, f32[32,256]{1,0:T(8,128)S(1)} %get-tuple-element.910, f32[32,256]{1,0:T(8,128)S(1)} %get-tuple-element.911, f32[32,256]{1,0:T(8,128)S(1)} %get-tuple-element.912, ...), kind=kLoop, calls=%fused_computation.8.clone.1 | loop fusion | flops 23060480 | bytes 262144 | tf_op jit(solution)/shard_map/while/body/eval_jaxpr/while/body/eval_jaxpr/reduce_sum | solution.py:53
  327.3 5.3 %multiply_reduce_fusion.13 = f32[32,256]{1,0:T(8,128)S(1)} fusion(f32[32,256]{1,0:T(8,128)S(1)} %get-tuple-element.908, f32[32,256]{1,0:T(8,128)S(1)} %get-tuple-element.909, f32[32,256]{1,0:T(8,128)S(1)} %get-tuple-element.910, f32[32,256]{1,0:T(8,128)S(1)} %get-tuple-element.911, f32[32,256]{1,0:T(8,128)S(1)} %get-tuple-element.912, ...), kind=kLoop, calls=%fused_computation.8.clone.1 | loop fusion | flops 23060480 | bytes 262144 | tf_op jit(solution)/shard_map/while/body/eval_jaxpr/while/body/eval_jaxpr/reduce_sum | solution.py:53
  333.5 5.3 %multiply_reduce_fusion.13 = f32[32,256]{1,0:T(8,128)S(1)} fusion(f32[32,256]{1,0:T(8,128)S(1)} %get-tuple-element.908, f32[32,256]{1,0:T(8,128)S(1)} %get-tuple-element.909, f32[32,256]{1,0:T(8,128)S(1)} %get-tuple-element.910, f32[32,256]{1,0:T(8,128)S(1)} %get-tuple-element.911, f32[32,256]{1,0:T(8,128)S(1)} %get-tuple-element.912, ...), kind=kLoop, calls=%fused_computation.8.clone.1 | loop fusion | flops 23060480 | bytes 262144 | tf_op jit(solution)/shard_map/while/body/eval_jaxpr/while/body/eval_jaxpr/reduce_sum | solution.py:53
  339.7 5.3 %multiply_reduce_fusion.13 = f32[32,256]{1,0:T(8,128)S(1)} fusion(f32[32,256]{1,0:T(8,128)S(1)} %get-tuple-element.908, f32[32,256]{1,0:T(8,128)S(1)} %get-tuple-element.909, f32[32,256]{1,0:T(8,128)S(1)} %get-tuple-element.910, f32[32,256]{1,0:T(8,128)S(1)} %get-tuple-element.911, f32[32,256]{1,0:T(8,128)S(1)} %get-tuple-element.912, ...), kind=kLoop, calls=%fused_computation.8.clone.1 | loop fusion | flops 23060480 | bytes 262144 | tf_op jit(solution)/shard_map/while/body/eval_jaxpr/while/body/eval_jaxpr/reduce_sum | solution.py:53
  345.2 8.2 %gather_fusion.2 = f32[2048,256]{1,0:T(8,128)S(1)} fusion(f32[2048,256]{1,0:T(8,128)} %bitcast.16, s32[2048]{0:T(1024)S(1)} %copy-done.11), kind=kCustom, calls=%fused_computation.2 | custom fusion | bytes 4202496 | tf_op jit(solution)/shard_map/jit(_take)/gather | solution.py:117
  355.1 52.8 %while.68 = (s32[]{:T(128)}, f32[128,64]{0,1:T(8,128)S(1)}, f32[3,128,64]{1,2,0:T(8,128)S(1)}, f32[128,16,256]{2,1,0:T(8,128)}, f32[128,16]{0,1:T(8,128)}, /*index=5*/s32[]{:T(128)}, s32[]{:T(128)}) while((s32[]{:T(128)}, f32[128,64]{0,1:T(8,128)S(1)}, f32[3,128,64]{1,2,0:T(8,128)S(1)}, f32[128,16,256]{2,1,0:T(8,128)}, ...), condition=%wide.region_6.7_spmd.clone, body=%wide.region_4.6_spmd.clone.sunk | while | flops 5783555 | bytes 1345119 | solution.py:76
  408.0 6.4 %fusion.57 = f32[128,1,256]{2,1,0:T(1,128)S(1)} fusion(f32[128,64,1]{1,2,0:T(1,128)S(1)} %copy.201, f32[128,64,256]{2,1,0:T(8,128)} %param.24), kind=kOutput, calls=%fused_computation.200 | convolution fusion | flops 25165824 | bytes 8552448 | tf_op jit(solution)/shard_map/lrp,lr->lp/dot_general | solution.py:198
  (663 shorter events, 180.1 us)
Async XLA Ops:
  0.0 45.8 %copy-start = (f32[16,64,64]{2,1,0:T(8,128)S(1)}, f32[16,64,64]{2,1,0:T(8,128)}, u32[]{:S(2)}) copy-start(f32[16,64,64]{2,1,0:T(8,128)} %param.26) | copy-start | bytes 786436
  0.0 8.9 %copy-start.8 = (s32[16,16]{1,0:T(8,128)S(1)}, s32[16,16]{1,0:T(8,128)}, u32[]{:S(2)}) copy-start(s32[16,16]{1,0:T(8,128)} %param.32) | copy-start | bytes 3076
  0.0 22.6 %copy-start.14 = (s32[128,16]{0,1:T(8,128)S(1)}, s32[128,16]{0,1:T(8,128)}, u32[]{:S(2)}) copy-start(s32[128,16]{0,1:T(8,128)} %param.31) | copy-start | bytes 24580
  0.0 24.3 %copy-start.15 = (s32[2,16]{1,0:T(2,128)S(1)}, s32[2,16]{1,0:T(2,128)}, u32[]{:S(2)}) copy-start(s32[2,16]{1,0:T(2,128)} %param.33) | copy-start | bytes 388
  1.2 184.8 %collective-permute-start = (f32[128,1024]{1,0:T(8,128)S(1)}, f32[128,1024]{1,0:T(8,128)}, u32[]{:S(2)}, u32[]{:S(2)}) collective-permute-start(f32[128,1024]{1,0:T(8,128)S(1)} %bitcast.163), channel_id=1, source_target_pairs={{0,1},{1,2},{2,3},{3,4},{4,5},{5,6},{6,7},{7,8},{8,9},{9,10},{10,1... | collective-permute-start | bytes 1572872 | tf_op jit(solution)/shard_map/ppermute | solution.py:18
  5.2 180.8 %collective-permute-start.1 = (f32[128,1024]{1,0:T(8,128)S(1)}, f32[128,1024]{1,0:T(8,128)}, u32[]{:S(2)}, u32[]{:S(2)}) collective-permute-start(f32[128,1024]{1,0:T(8,128)S(1)} %bitcast.164), channel_id=1, source_target_pairs={{1,0},{2,1},{3,2},{4,3},{5,4},{6,5},{7,6},{8,7},{9,8},{10,9},{11,1... | collective-permute-start | bytes 1572872 | tf_op jit(solution)/shard_map/ppermute | solution.py:20
  12.9 51.5 %all-to-all-start.2 = ((s32[128,1,2]{2,1,0:T(1,128)}), s32[128,1,2]{2,1,0:T(1,128)S(1)}, u32[]{:S(2)}, u32[]{:S(2)}) async-start(s32[128,1,2]{2,1,0:T(1,128)} %bitcast.24), calls=%async_computation.2 | async-start | bytes 131072 | tf_op jit(solution)/shard_map/all_to_all | solution.py:112
  29.9 13.5 %copy-start.3 = (f32[3,128,64]{1,2,0:T(8,128)S(1)}, f32[3,128,64]{1,2,0:T(8,128)}, u32[]{:S(2)}) copy-start(f32[3,128,64]{1,2,0:T(8,128)} %param.27) | copy-start | bytes 294916
  29.9 14.2 %copy-start.1 = (f32[128,64,64]{0,2,1:T(8,128)S(1)}, f32[128,64,64]{0,2,1:T(8,128)}, u32[]{:S(2)}) copy-start(f32[128,64,64]{0,2,1:T(8,128)} %param.25) | copy-start | bytes 6291460
  40.5 9.6 %copy-start.4 = (f32[3,16,64]{2,1,0:T(8,128)S(1)}, f32[3,16,64]{2,1,0:T(8,128)}, u32[]{:S(2)}) copy-start(f32[3,16,64]{2,1,0:T(8,128)} %param.28) | copy-start | bytes 36868
  40.5 9.6 %copy-start.9 = (f32[3,2,64]{2,1,0:T(2,128)S(1)}, f32[3,2,64]{2,1,0:T(2,128)}, u32[]{:S(2)}) copy-start(f32[3,2,64]{2,1,0:T(2,128)} %param.29) | copy-start | bytes 4612
  43.4 2.4 copy-start.12
  64.5 19.5 %all-to-all-start = ((s32[128,1,16]{2,1,0:T(1,128)}), s32[128,1,16]{2,1,0:T(1,128)S(1)}, u32[]{:S(2)}, u32[]{:S(2)}) async-start(s32[128,1,16]{2,1,0:T(1,128)} %bitcast.8), calls=%async_computation | async-start | bytes 131072 | tf_op jit(solution)/shard_map/all_to_all | solution.py:112
  84.7 16.2 %all-to-all-start.4 = ((f32[128,2,256]{2,1,0:T(2,128)}), f32[128,2,256]{2,1,0:T(2,128)}, u32[]{:S(2)}, u32[]{:S(2)}) async-start(f32[128,2,256]{2,1,0:T(2,128)} %stack.3), calls=%async_computation.4 | async-start | bytes 524288 | tf_op jit(solution)/shard_map/all_to_all | solution.py:162
  100.9 18.6 %all-to-all-start.3 = ((f32[128,2,256]{2,1,0:T(2,128)}), f32[128,2,256]{2,1,0:T(2,128)S(1)}, u32[]{:S(2)}, u32[]{:S(2)}) async-start(f32[128,2,256]{2,1,0:T(2,128)} %broadcast_select_fusion.3), calls=%async_computation.3 | async-start | bytes 524288 | tf_op jit(solution)/shard_map/all_to_all | solution.py:115
  119.5 225.6 %all-to-all-start.1 = ((f32[128,16,256]{2,1,0:T(8,128)}), f32[128,16,256]{2,1,0:T(8,128)}, u32[]{:S(2)}, u32[]{:S(2)}) async-start(f32[128,16,256]{2,1,0:T(8,128)} %broadcast_select_fusion.2), calls=%async_computation.1 | async-start | bytes 4194304 | tf_op jit(solution)/shard_map/all_to_all | solution.py:115
  127.6 2.1 copy-start.13
  127.8 58.0 %copy-start.2 = (f32[128,64,64]{0,2,1:T(8,128)S(1)}, f32[128,64,64]{0,2,1:T(8,128)}, u32[]{:S(2)}) copy-start(f32[128,64,64]{0,2,1:T(8,128)} %param.25) | copy-start | bytes 6291460
  186.0 1.4 copy-start.5
  186.0 1.4 copy-start.6
  186.0 1.4 copy-start.7
  187.4 157.7 %copy-start.11 = (s32[2048]{0:T(1024)S(1)}, s32[2048]{0:T(1024)}, u32[]{:S(2)}) copy-start(s32[2048]{0:T(1024)} %broadcast_clamp_fusion) | copy-start | bytes 24580
  345.1 8.3 %copy-start.10 = (pred[128,16]{1,0:T(8,128)(4,1)S(1)}, pred[128,16]{1,0:T(8,128)(4,1)}, u32[]{:S(2)}) copy-start(pred[128,16]{1,0:T(8,128)(4,1)} %get-tuple-element.658) | copy-start | bytes 6148
